TPU v7x, 512 devices: a whole 4x8x8 slice. The times are simulated.
512 devices in a mesh: feat: 32 (over x, z), tok: 16 (over y, core).
Axes of the slice: x: 4, y: 8, z: 8, core: 2. Of those that a mesh axis runs over, the one named last changes fastest.
Arguments:
- activations: bfloat16 [2048, 8192], P('tok', 'feat'), may hold values from -6 to 6
- w_base: bfloat16 [8192, 8192], P('feat', 'tok'), may hold values from -0.0625 to 0.0625
- blk_vals: bfloat16 [96, 128, 128], P('feat'), may hold values from -0.5 to 0.5
- blk_index: int32 [96, 2], P('feat'), may hold values from 0 to 63, as said below
- blk_count: int32 [32], P('feat'), may hold values from 1 to 3, as said below
- a_down: bfloat16 [8192, 64], P('feat'), may hold values from -0.0625 to 0.0625
- b_up: bfloat16 [64, 8192], P(None, 'feat'), may hold values from -0.75 to 0.75
- grad_out: bfloat16 [2048, 8192], P('tok', 'feat'), may hold values from -6 to 6
Outputs:
- projected: bfloat16 [2048, 8192], P('tok', 'feat')
- grad_x: bfloat16 [2048, 8192], P('tok', 'feat')
- grad_blocks: float32 [96, 128, 128], P('feat')
- grad_a: float32 [8192, 64], P('feat')
- grad_b: float32 [64, 8192], P(None, 'feat')
Inputs may be any that keep to these rules, and one draw needn't show every extreme that they name: `blk_index`: column 0 is below 2 and column 1 below 64; both largest values occur in every draw. `blk_count`: some feature shard holds exactly 3 live slots in every draw.
All inputs are finite; a program needn't handle non-finite values.
Results may differ from a plain program's by a relative error of at most 0.014.
Values may be sent and summed in bfloat16 or wider, within the bound.
A program may use at most 64 MiB of HBM per device.

v0:
```python
import jax
import jax.numpy as jnp
from jax import lax
from jax.sharding import PartitionSpec as P

BLK = 128


def on_device(activations, w_base, blk_vals, blk_index, blk_count, a_down, b_up, grad_out):
    tok_rows = activations.shape[0]
    grad_scale = float(tok_rows * lax.axis_size("tok")) ** (-0.5)
    live_count = blk_count[0]
    u_part = jnp.dot(activations, a_down, preferred_element_type=jnp.float32)
    v_part = jnp.dot(grad_out, b_up.T, preferred_element_type=jnp.float32)
    u_total = lax.psum(u_part, "feat")
    u_half = u_total.astype(jnp.bfloat16)
    w_rows = lax.all_gather(w_base, "tok", axis=1, tiled=True)
    partial_value = jnp.dot(activations, w_rows, preferred_element_type=jnp.float32)
    for slot_idx in range(blk_vals.shape[0]):
        is_live = (slot_idx < live_count).astype(jnp.float32)
        row_start = blk_index[slot_idx, 0] * BLK
        col_start = blk_index[slot_idx, 1] * BLK
        x_cols = lax.dynamic_slice_in_dim(activations, row_start, BLK, 1)
        forward_add = (
            jnp.dot(x_cols, blk_vals[slot_idx], preferred_element_type=jnp.float32) * is_live
        )
        current = lax.dynamic_slice_in_dim(partial_value, col_start, BLK, 1)
        partial_value = lax.dynamic_update_slice_in_dim(
            partial_value, current + forward_add, col_start, 1
        )
    own_sums = lax.psum_scatter(
        partial_value.astype(jnp.bfloat16), "feat", scatter_dimension=1, tiled=True
    ).astype(jnp.float32)
    projected = (own_sums + jnp.dot(u_half, b_up, preferred_element_type=jnp.float32)).astype(
        jnp.bfloat16
    )
    v_total = lax.psum(v_part, "feat")
    v_half = v_total.astype(jnp.bfloat16)
    cot_rows = lax.all_gather(grad_out, "feat", axis=1, tiled=True)
    backward = jnp.dot(cot_rows, w_rows.T, preferred_element_type=jnp.float32)
    block_terms = []
    for slot_idx in range(blk_vals.shape[0]):
        is_live = (slot_idx < live_count).astype(jnp.float32)
        row_start = blk_index[slot_idx, 0] * BLK
        col_start = blk_index[slot_idx, 1] * BLK
        x_cols = lax.dynamic_slice_in_dim(activations, row_start, BLK, 1)
        g_cols = lax.dynamic_slice_in_dim(cot_rows, col_start, BLK, 1)
        back_add = (
            jnp.dot(g_cols, blk_vals[slot_idx].T, preferred_element_type=jnp.float32) * is_live
        )
        current = lax.dynamic_slice_in_dim(backward, row_start, BLK, 1)
        backward = lax.dynamic_update_slice_in_dim(backward, current + back_add, row_start, 1)
        block_terms.append(jnp.dot(x_cols.T, g_cols, preferred_element_type=jnp.float32) * is_live)
    grad_x = (backward + jnp.dot(v_half, a_down.T, preferred_element_type=jnp.float32)).astype(
        jnp.bfloat16
    )
    block_local = jnp.stack(block_terms, axis=0)
    down_local = jnp.dot(activations.T, v_half, preferred_element_type=jnp.float32)
    up_local = jnp.dot(u_half.T, grad_out, preferred_element_type=jnp.float32)
    block_sum, down_sum, up_sum = lax.psum((block_local, down_local, up_local), "tok")
    return (projected, grad_x, block_sum * grad_scale, down_sum * grad_scale, up_sum * grad_scale)


def solution(mesh):
    in_specs = (
        P("tok", "feat"),
        P("feat", "tok"),
        P("feat", None, None),
        P("feat", None),
        P("feat"),
        P("feat", None),
        P(None, "feat"),
        P("tok", "feat"),
    )
    out_specs = (
        P("tok", "feat"),
        P("tok", "feat"),
        P("feat", None, None),
        P("feat", None),
        P(None, "feat"),
    )
    return jax.shard_map(
        on_device, mesh=mesh, in_specs=in_specs, out_specs=out_specs, check_vma=False
    )
```

profile of v0, /device:TPU:1, one launch (start us, length us, event | category | flops | bytes accessed | tf_op | source)
XLA Modules:
  0.0 513.2 jit_solution(15335018569101038187)
XLA Ops:
  7.2 0.0 copy-start
  7.2 0.0 all-gather.5.cloned.1.call-start
  7.2 0.7 all-gather.5.cloned.1.call-update
  7.9 0.0 all-gather.3.cloned.1.call-start
  8.0 0.7 all-gather.3.cloned.1.call-update
  8.7 0.0 all-reduce.4.cloned.1.call-start
  8.7 1.6 fusion.55
  14.9 1.0 fusion.59
  15.9 0.0 copy-done
  15.9 0.9 fusion.57
  16.8 122.8 %all-reduce = (bf16[128,64]{0,1:T(8,128)(2,1)S(1)}, bf16[128,64]{0,1:T(8,128)(2,1)S(1)}) all-reduce(f32[128,64]{0,1:T(8,128)S(1)} %fusion.57, f32[128,64]{0,1:T(8,128)S(1)} %fusion.59), channel_id=1, replica_groups=mesh['feat'=32,'tok'=16] {'feat'}, use_global_device_ids=true, to_apply=%region_1.0 | all-reduce | flops 16384 | bytes 98304 | tf_op jit(solution)/shard_map/psum | solution.py:15
  139.6 1.6 fusion.60
  141.2 0.8 convolution_bitcast_fusion
  142.0 0.0 all-gather.5.cloned.1.call-done
  142.0 0.9 fusion.2
  142.9 0.9 fusion.3
  143.9 0.9 fusion.4
  144.8 0.7 pad_maximum_fusion
  145.5 0.0 all-reduce.4.cloned.1.call-update
  145.5 0.0 copy-start.2
  145.6 0.0 reduce-scatter.2.cloned.1.call-start
  145.6 0.0 all-gather.3.cloned.1.call-done
  145.6 2.9 fusion.56
  148.6 0.0 copy-done.2
  148.6 0.1 fusion.16
  148.7 0.1 fusion.14
  148.8 0.1 fusion.12
  149.0 0.0 copy-start.1
  149.0 1.6 convert_element_type.45
  150.6 0.0 reduce-scatter.2.cloned.1.call-update
  150.6 0.0 copy-start.3
  150.6 0.0 copy-start.4
  150.6 130.1 %all-reduce.4.cloned.1.call-done = (f32[3,128,128]{2,1,0:T(8,128)}, f32[256,64]{0,1:T(8,128)}, f32[64,256]{1,0:T(8,128)}) async-done(((f32[3,128,128]{2,1,0:T(8,128)}, f32[256,64]{0,1:T(8,128)}, f32[64,256]{1,0:T(8,128)}), (f32[3,128,128]{2,1,0:T(8,128)}, f32[256,64]{0,1:T(8,128)}, f32[64,256]{1,0:T(8,128)})) %all-reduce.4.cloned.1.call-update) | async-done | bytes 327696 | tf_op jit(solution)/shard_map/psum | solution.py:60
  280.8 1.5 broadcast_multiply_fusion.2
  282.2 1.5 broadcast_multiply_fusion.1
  283.7 1.6 broadcast_multiply_fusion
  285.3 0.0 copy-done.1
  285.3 3.7 fusion.58
  289.1 0.1 fusion.10
  289.2 0.2 fusion.8
  289.4 0.2 fusion.6
  289.5 0.0 copy-done.3
  289.5 0.8 fusion.1
  290.4 214.6 %reduce-scatter.2.cloned.1.call-done = bf16[128,256]{1,0:T(8,128)(2,1)} async-done(((bf16[128,8192]{1,0:T(8,128)(2,1)}), bf16[128,256]{1,0:T(8,128)(2,1)}) %reduce-scatter.2.cloned.1.call-update) | async-done | bytes 65552 | tf_op jit(solution)/shard_map/reduce_scatter | solution.py:31
  505.0 0.0 copy-done.4
  505.0 1.7 fusion
Async XLA Ops:
  7.2 8.7 %copy-start = (bf16[128,256]{1,0:T(8,128)(2,1)S(1)}, bf16[128,256]{1,0:T(8,128)(2,1)}, u32[]{:S(2)}) copy-start(bf16[128,256]{1,0:T(8,128)(2,1)} %param.8) | copy-start | bytes 196612
  7.2 134.8 %all-gather.5.cloned.1.call-start = ((), (), s32[]{:S(2)}) async-start(), calls=%async_computation.3 | async-start | bytes 2162688 | tf_op jit(solution)/shard_map/all_gather | solution.py:39
  7.9 137.7 %all-gather.3.cloned.1.call-start = ((), (), s32[]{:S(2)}) async-start(), calls=%async_computation.1 | async-start | bytes 4456448 | tf_op jit(solution)/shard_map/all_gather | solution.py:17
  8.7 272.1 %all-reduce.4.cloned.1.call-start = ((), (), s32[]{:S(2)}) async-start(), calls=%async_computation.4 | async-start | bytes 655360 | tf_op jit(solution)/shard_map/psum | solution.py:60
  145.5 3.0 copy-start.2
  145.6 359.4 %reduce-scatter.2.cloned.1.call-start = ((), (), s32[]{:S(2)}) async-start(), calls=%async_computation.2 | async-start | bytes 2162688 | tf_op jit(solution)/shard_map/reduce_scatter | solution.py:31
  149.0 136.4 %copy-start.1 = (bf16[128,8192]{1,0:T(8,128)(2,1)S(1)}, bf16[128,8192]{1,0:T(8,128)(2,1)}, u32[]{:S(2)}) copy-start(bf16[128,8192]{1,0:T(8,128)(2,1)} %all-gather.5.cloned.1.call-done) | copy-start | bytes 6291460
  150.6 138.9 %copy-start.3 = (bf16[256,64]{0,1:T(8,128)(2,1)S(1)}, bf16[256,64]{0,1:T(8,128)(2,1)}, u32[]{:S(2)}) copy-start(bf16[256,64]{0,1:T(8,128)(2,1)} %param.13) | copy-start | bytes 98308
  150.6 354.4 %copy-start.4 = (bf16[64,256]{1,0:T(8,128)(2,1)S(1)}, bf16[64,256]{1,0:T(8,128)(2,1)}, u32[]{:S(2)}) copy-start(bf16[64,256]{1,0:T(8,128)(2,1)} %param.14) | copy-start | bytes 98308
Sparse Core Ops, SparseCore 0:
  11.0 82.6 all-gather.4
  95.9 47.2 all-gather.2
  146.3 134.4 all-reduce.3
  285.0 219.9 reduce-scatter.1
where the time goes:
time: 518 us; the launch traced here: 513 us
  waiting for transfers between devices  346 us (67%)
  blocking collectives  123 us (24%)
  between operations  18.5 us (4%)
  matrix products  17.1 us (3%)
  other arithmetic  6.85 us (1%)
    reduce_scatter x1, waiting for transfers between devices, on_device(): lax.psum_scatter(partial_value.astype(jnp.bfloat16), 'feat', scatter_dime...  215 us
    psum x1, waiting for transfers between devices, on_device(): lax.psum((block_local, down_local, up_local), 'tok')  130 us
    psum x1, blocking collectives, on_device(): u_total = lax.psum(u_part, 'feat')  123 us
  transfers between devices with their start and end apart: 4, of which 2 were waited for; matrix products, arithmetic and copies ran while one was open for 5% of the time, Pallas kernels for 0%

commit v1 on v0

v1 whole, which is shorter than its diff:
```python
import functools

import jax
import jax.numpy as jnp
from jax import lax
from jax.experimental import pallas as pl
from jax.experimental.pallas import tpu as pltpu
from jax.sharding import PartitionSpec as P

MESH = pl.DeviceIdType.MESH
F32 = jnp.float32
BF16 = jnp.bfloat16
BLK = 128
NC = 2


def dot(a, b, ca, cb):
    return lax.dot_general(a, b, (((ca,), (cb,)), ((), ())), preferred_element_type=F32)


def kernel(
    dims, scale,
    x_ref, w_ref, blk_ref, idx_ref, at_ref, b_ref, g_ref,
    proj_ref, gradx_ref, grada_ref, gradb_ref, gradblk_ref,
    wl, wq, xg, gz, orx, os_, gxr, gxs, gxacc, uvx, uvz, uvt, idxg, bs, br, rss, rsr, agb, ab, gab,
    ring_s, ring_r, fwd_s, fwd_r, x_s, x_r, g_s, g_r, o_s, o_r, q_s, q_r,
    ux_s, ux_r, uz_s, uz_r, id_s, id_r, b_s, b_r, rs_s, rs_r, ag_s, ag_r,
):
    nx, ny, nz = dims
    nq = ny // nx
    nt = ny * NC
    half = ny // 2
    feat, tok = lax.axis_index("feat"), lax.axis_index("tok")
    x, z = feat // nz, feat % nz
    y, c = tok // NC, tok % NC
    zc = (z // 2) % 2
    zq, zh = z // (2 * NC), z % 2
    sib = 1 - c
    hb = x_ref.shape[0]
    pending = []

    def dev(xx, yy, zz, cc):
        return (xx * nz + zz, yy * NC + cc)

    def send(src, dst, s_sem, r_sem, target):
        copy = pltpu.make_async_remote_copy(
            src_ref=src, dst_ref=dst, send_sem=s_sem, recv_sem=r_sem, device_id=target, device_id_type=MESH
        )
        copy.start()
        pending.append((None, copy))

    def send_or_keep(mine, src, dst, s_sem, r_sem, target):
        @pl.when(mine)
        def _():
            pltpu.make_async_copy(src, dst, r_sem).start()

        copy = pltpu.make_async_remote_copy(
            src_ref=src, dst_ref=dst, send_sem=s_sem, recv_sem=r_sem, device_id=target, device_id_type=MESH
        )

        @pl.when(jnp.logical_not(mine))
        def _():
            copy.start()

        pending.append((mine, copy))

    def arrived(dst, sem):
        pltpu.make_async_copy(dst, dst, sem).wait()

    barrier = pltpu.get_barrier_semaphore()
    greeted = 0
    for dx in range(1, nx):
        for cc in range(NC):
            pl.semaphore_signal(barrier, inc=1, device_id=dev((x + dx) % nx, y, z, cc), device_id_type=MESH)
            greeted += 1
    for dz in range(1, nz):
        for cc in range(NC):
            pl.semaphore_signal(barrier, inc=1, device_id=dev(x, y, (z + dz) % nz, cc), device_id_type=MESH)
            greeted += 1
    for dt in range(1, nt):
        pl.semaphore_signal(barrier, inc=1, device_id=(feat, (tok + dt) % nt), device_id_type=MESH)
        greeted += 1

    nsl = blk_ref.shape[0]
    for h in range(2):
        for rr in range(2):
            for hh in range(2):
                r0, c0 = rr * BLK, h * 2 * BLK + hh * BLK
                piece = w_ref[r0:r0 + BLK, c0:c0 + BLK].astype(F32)
                column = (tok * 4 + h * 2 + hh).astype(F32)
                for j in range(nsl):
                    hit = jnp.where(idx_ref[j:j + 1, :] == column, 1.0, 0.0) * jnp.where(
                        idx_ref[4 + j:5 + j, :] == float(rr), 1.0, 0.0
                    )
                    piece = piece + hit * blk_ref[j].astype(F32)
                wl[0, h, r0:r0 + BLK, hh * BLK:(hh + 1) * BLK] = piece.astype(BF16)

    rank = at_ref.shape[0]
    ab[...] = jnp.zeros_like(ab)
    ab[0, 0:rank, :] = at_ref[...]
    ab[1, rank:2 * rank, :] = b_ref[...]
    ab[2, 0:rank, :] = b_ref[...]
    ab[3, rank:2 * rank, :] = at_ref[...]
    uvx[x] = (dot(x_ref[...], ab[0], 1, 1) + dot(g_ref[...], ab[1], 1, 1)).astype(BF16)
    idxg[x] = idx_ref[...]

    pl.semaphore_wait(barrier, greeted)

    last = ny - 2

    def ring_slot(direction, k):
        d, sub = k // 2 + 1, (k + direction) % 2
        return (d if direction == 0 else half + d), d, sub

    def ring_send(direction, k):
        if k > last:
            return
        if k < 2:
            src = wl.at[0, (k + direction) % 2]
        else:
            slot, _, sub = ring_slot(direction, k - 2)
            src = wl.at[slot, sub]
        slot, _, sub = ring_slot(direction, k)
        to = (y + 1) % ny if direction == 0 else (y + ny - 1) % ny
        send(src, wl.at[slot, sub], ring_s.at[direction, k], ring_r.at[direction, k], dev(x, to, z, c))

    def hand_on(slot, sub, yy):
        xx, qq = yy // nq, yy % nq
        send_or_keep(x == xx, wl.at[slot, sub], wq.at[x, qq, sub], fwd_s.at[slot, sub], fwd_r.at[x, qq, sub], dev(xx, y, z, c))

    def ring_step(k):
        for direction in range(2):
            slot, d, sub = ring_slot(direction, k)
            arrived(wl.at[slot, sub], ring_r.at[direction, k])
            ring_send(direction, k + 2)
            yy = (y + ny - d) % ny if direction == 0 else (y + d) % ny
            hand_on(slot, sub, yy)

    for k in range(2):
        for direction in range(2):
            ring_send(direction, k)
    for dx in range(1, nx):
        send(uvx.at[x], uvx.at[x], ux_s.at[dx], ux_r.at[x], dev((x + dx) % nx, y, z, c))
    for dx in range(nx):
        for cc in range(NC):
            own = c == cc if dx == 0 else None
            rows = pl.ds(pl.multiple_of(c * hb, hb), hb)
            args = (x_ref, xg.at[x, rows], x_s.at[dx, cc], x_r.at[x, c], dev((x + dx) % nx, y, z, cc))
            if own is None:
                send(*args)
            else:
                send_or_keep(own, *args)
    for dx in range(1, nx):
        send(idxg.at[x], idxg.at[x], id_s.at[dx], id_r.at[x], dev((x + dx) % nx, y, z, c))
    for dz in range(nz):
        rows = pl.ds(pl.multiple_of(c * hb, hb), hb)
        args = (g_ref, gz.at[zq, zh, rows], g_s.at[dz], g_r.at[zq, zh, c], dev(x, y, (z + dz) % nz, zc))
        if dz:
            send(*args)
        else:
            send_or_keep(c == zc, *args)
    for h in range(2):
        hand_on(0, h, y)

    def low_rank_over_z():
        total = uvx[x].astype(F32)
        for dx in range(1, nx):
            xx = (x + dx) % nx
            arrived(uvx.at[xx], ux_r.at[xx])
            total = total + uvx[xx].astype(F32)
        uvz[z] = total.astype(BF16)
        for dz in range(1, nz):
            send(uvz.at[z], uvz.at[z], uz_s.at[dz], uz_r.at[z], dev(x, y, (z + dz) % nz, c))

    def low_rank_done():
        total = uvz[z].astype(F32)
        for dz in range(1, nz):
            zz = (z + dz) % nz
            arrived(uvz.at[zz], uz_r.at[zz])
            total = total + uvz[zz].astype(F32)
        uvt[...] = total.astype(BF16)

    def blocks_over_x():
        for dx in range(nx):
            xx = (x + dx) % nx
            if dx:
                arrived(idxg.at[xx], id_r.at[xx])
            for cc in range(NC):
                arrived(xg.at[xx, cc * hb:(cc + 1) * hb], x_r.at[xx, cc])
        for qq in range(nq):
            for h in range(2):
                for cc in range(NC):
                    arrived(gz.at[qq, h, cc * hb:(cc + 1) * hb], g_r.at[qq, h, cc])
        for dx in range(nx):
            xx = (x + dx) % nx
            for j in range(nsl):
                col, row = idxg[xx, j:j + 1, :], idxg[xx, 4 + j:5 + j, :]
                picked = jnp.zeros((NC * hb, BLK), BF16)
                for qq in range(nq):
                    for h in range(2):
                        base = (2 * (x * nz + 4 * qq + 2 * c + h)).astype(F32)
                        for hh in range(2):
                            hit = jnp.where(col == base + float(hh), 1.0, 0.0).astype(BF16)
                            picked = picked + gz[qq, h, :, hh * BLK:(hh + 1) * BLK] * hit
                top = jnp.where(row == 0.0, 1.0, 0.0).astype(BF16)
                low = jnp.where(row == 1.0, 1.0, 0.0).astype(BF16)
                xs = xg[xx, :, 0:BLK] * top + xg[xx, :, BLK:2 * BLK] * low
                bs[dx, j * BLK:(j + 1) * BLK, :] = dot(xs, picked, 0, 0).astype(BF16)
            if dx:
                send(bs.at[dx], br.at[x], b_s.at[dx], b_r.at[x], dev(xx, y, z, c))

    ra, rb = 2 * rank // nt, nsl * BLK // nt

    def grads_over_tok():
        uv = uvt[...]
        gab[0:rank] = dot(uv, g_ref[...], 0, 0)[0:rank]
        gab[rank:2 * rank] = dot(uv, x_ref[...], 0, 0)[rank:2 * rank]
        for dx in range(1, nx):
            xx = (x + dx) % nx
            arrived(br.at[xx], b_r.at[xx])
        for tt in range(nt):
            rss[tt, 0:ra, :] = gab[tt * ra:(tt + 1) * ra, 0:BLK]
            rss[tt, ra:2 * ra, :] = gab[tt * ra:(tt + 1) * ra, BLK:2 * BLK]
        blk_sum = bs[0].astype(F32)
        for dx in range(1, nx):
            blk_sum = blk_sum + br[(x + dx) % nx].astype(F32)
        for tt in range(nt):
            rss[tt, 2 * ra:2 * ra + rb, :] = blk_sum[tt * rb:(tt + 1) * rb]
        rsr[tok] = rss[tok]
        for dt in range(1, nt):
            tt = (tok + dt) % nt
            send(rss.at[tt], rsr.at[tok], rs_s.at[dt], rs_r.at[tok], (feat, tt))

    def grads_back():
        total = rsr[tok]
        for dt in range(1, nt):
            tt = (tok + dt) % nt
            arrived(rsr.at[tt], rs_r.at[tt])
            total = total + rsr[tt]
        agb[tok] = total * scale
        for dt in range(1, nt):
            send(agb.at[tok], agb.at[tok], ag_s.at[dt], ag_r.at[tok], (feat, (tok + dt) % nt))

    side = [low_rank_over_z, low_rank_done, blocks_over_x, grads_over_tok, grads_back]
    for k in range(ny - 1):
        ring_step(k)
        if side:
            side.pop(0)()
    for step in side:
        step()

    for j in range(2 * nq):
        qq, h = j // 2, j % 2
        for dx in range(nx):
            xx = (x + dx) % nx
            arrived(wq.at[xx, qq, h], fwd_r.at[xx, qq, h])
        out = dot(xg[0], wq[0, qq, h], 1, 0)
        for xx in range(1, nx):
            out = out + dot(xg[xx], wq[xx, qq, h], 1, 0)
        os_[j] = out.astype(BF16)
        zz = 4 * qq + 2 * c + h
        for cc in range(NC):
            send_or_keep(
                jnp.logical_and(z == zz, c == cc),
                os_.at[j, cc * hb:(cc + 1) * hb], orx.at[z], o_s.at[j, cc], o_r.at[z], dev(x, y, zz, cc),
            )
        for xx in range(nx):
            term = dot(gz[qq, h], wq[xx, qq, h], 1, 1)
            gxacc[xx] = term if j == 0 else gxacc[xx] + term
    for dx in range(nx):
        xx = (x + dx) % nx
        gxs[dx] = gxacc[xx].astype(BF16)
        for cc in range(NC):
            args = (gxs.at[dx, cc * hb:(cc + 1) * hb], gxr.at[x, c], q_s.at[dx, cc], q_r.at[x, c], dev(xx, y, z, cc))
            if dx:
                send(*args)
            else:
                send_or_keep(c == cc, *args)

    uv = uvt[...]
    out = dot(uv, ab[2], 1, 0)
    for zz in range(nz):
        arrived(orx.at[zz], o_r.at[zz])
        out = out + orx[zz].astype(F32)
    proj_ref[...] = out.astype(BF16)

    for dt in range(1, nt):
        tt = (tok + dt) % nt
        arrived(agb.at[tt], ag_r.at[tt])
    for tt in range(nt):
        r0 = tt * ra
        ref, r0 = (gradb_ref, r0) if r0 < rank else (grada_ref, r0 - rank)
        ref[r0:r0 + ra, 0:BLK] = agb[tt, 0:ra, :]
        ref[r0:r0 + ra, BLK:2 * BLK] = agb[tt, ra:2 * ra, :]
        gradblk_ref[tt * rb:(tt + 1) * rb, :] = agb[tt, 2 * ra:2 * ra + rb, :]

    out = dot(uv, ab[3], 1, 0)
    for xx in range(nx):
        for cc in range(NC):
            arrived(gxr.at[xx, cc], q_r.at[xx, cc])
            out = out + gxr[xx, cc].astype(F32)
    gradx_ref[...] = out.astype(BF16)

    for mine, copy in pending:
        if mine is None:
            copy.wait_send()
        else:
            pl.when(jnp.logical_not(mine))(copy.wait_send)


def make(dims):
    nx, ny, nz = dims
    nq, nt = ny // nx, ny * NC

    def on_device(activations, w_base, blk_vals, blk_index, blk_count, a_down, b_up, grad_out):
        hb, fb = activations.shape
        nsl, rank = blk_vals.shape[0], a_down.shape[1]
        scale = float(hb * nt) ** (-0.5)
        live = jnp.arange(nsl, dtype=jnp.int32) < blk_count[0]
        column = jnp.where(live, blk_index[:, 1], -1).astype(F32)
        table = jnp.zeros((8,), F32).at[0:nsl].set(column).at[4:4 + nsl].set(blk_index[:, 0].astype(F32))
        table = jnp.broadcast_to(table[:, None], (8, BLK))
        piece = 2 * (2 * rank // nt) + nsl * BLK // nt
        dma = pltpu.SemaphoreType.DMA
        vmem = pltpu.VMEM
        proj, gradx, grad_at, grad_b, blk = pl.pallas_call(
            functools.partial(kernel, dims, scale),
            out_shape=[
                jax.ShapeDtypeStruct((hb, fb), BF16),
                jax.ShapeDtypeStruct((hb, fb), BF16),
                jax.ShapeDtypeStruct((rank, fb), F32),
                jax.ShapeDtypeStruct((rank, fb), F32),
                jax.ShapeDtypeStruct((nsl * BLK, BLK), F32),
            ],
            in_specs=[pl.BlockSpec(memory_space=vmem)] * 7,
            out_specs=[pl.BlockSpec(memory_space=vmem)] * 5,
            scratch_shapes=[
                vmem((ny + 1, 2, fb, fb), BF16),
                vmem((nx, nq, 2, fb, fb), BF16),
                vmem((nx, NC * hb, fb), BF16),
                vmem((nq, 2, NC * hb, fb), BF16),
                vmem((nz, hb, fb), BF16),
                vmem((2 * nq, NC * hb, fb), BF16),
                vmem((nx, NC, hb, fb), BF16),
                vmem((nx, NC * hb, fb), BF16),
                vmem((nx, NC * hb, fb), F32),
                vmem((nx, hb, 2 * rank), BF16),
                vmem((nz, hb, 2 * rank), BF16),
                vmem((hb, 2 * rank), BF16),
                vmem((nx, 8, BLK), F32),
                vmem((nx, nsl * BLK, BLK), BF16),
                vmem((nx, nsl * BLK, BLK), BF16),
                vmem((nt, piece, BLK), F32),
                vmem((nt, piece, BLK), F32),
                vmem((nt, piece, BLK), F32),
                vmem((4, 2 * rank, fb), BF16),
                vmem((2 * rank, fb), F32),
                dma((2, ny)), dma((2, ny)),
                dma((ny + 1, 2)), dma((nx, nq, 2)),
                dma((nx, NC)), dma((nx, NC)),
                dma((nz,)), dma((nq, 2, NC)),
                dma((2 * nq, NC)), dma((nz,)),
                dma((nx, NC)), dma((nx, NC)),
                dma((nx,)), dma((nx,)),
                dma((nz,)), dma((nz,)),
                dma((nx,)), dma((nx,)),
                dma((nx,)), dma((nx,)),
                dma((nt,)), dma((nt,)),
                dma((nt,)), dma((nt,)),
            ],
            compiler_params=pltpu.CompilerParams(
                collective_id=0, has_side_effects=True, vmem_limit_bytes=40 * 1024 * 1024
            ),
        )(activations, w_base, blk_vals, table, a_down.T, b_up, grad_out)
        return proj, gradx, blk.reshape(nsl, BLK, BLK), grad_at.T, grad_b

    return on_device


def solution(mesh, dims=(4, 8, 8)):
    in_specs = (
        P("tok", "feat"),
        P("feat", "tok"),
        P("feat", None, None),
        P("feat", None),
        P("feat"),
        P("feat", None),
        P(None, "feat"),
        P("tok", "feat"),
    )
    out_specs = (
        P("tok", "feat"),
        P("tok", "feat"),
        P("feat", None, None),
        P("feat", None),
        P(None, "feat"),
    )
    return jax.shard_map(make(dims), mesh=mesh, in_specs=in_specs, out_specs=out_specs, check_vma=False)
```

time: 518 us -> 104 us (0.20)
  waiting for transfers between devices: 346 us -> 0 us
  blocking collectives: 123 us -> 0 us
  Pallas kernels: 0 us -> 92.9 us
  between operations: 18.5 us -> 1.3 us
  matrix products: 17.1 us -> 0 us
  local copies, waits for them, and re-layouts: 1.63 us -> 8.98 us
  other arithmetic: 6.85 us -> 0.09 us
    reduce_scatter x1 -> x0, waiting for transfers between devices: 215 us -> none  [on_device(): lax.psum_scatter(partial_value.astype(jnp.bfloat16), 'feat', scatter_dime...]
    psum x1 -> x0, waiting for transfers between devices: 130 us -> none  [on_device(): lax.psum((block_local, down_local, up_local), 'tok')]
    psum x1 -> x0, blocking collectives: 123 us -> none  [on_device(): u_total = lax.psum(u_part, 'feat')]
    pallas_call x0 -> x1, Pallas kernels: none -> 92.9 us  [on_device(): pl.pallas_call(functools.partial(kernel, dims, scale), out_shape=[jax.Sha...]
    dot_general x17 -> x0, matrix products: 17.1 us -> none  [the longest x1 3.72 us: on_device(): backward = jnp.dot(cot_rows, w_rows.T, preferred_element_type=jnp.float32)]
    unnamed x10 -> x19, local copies, waits for them, and re-layouts: 0.05 us -> 8.9 us
  transfers between devices with their start and end apart: 4 -> 0, of which waited for: 2 -> 0; matrix products, arithmetic and copies ran while one was open for 5% -> 0% of each run, Pallas kernels for 0% -> 0%
where the time goes in v1:
time: 104 us; the launch traced here: 103 us
  Pallas kernels  92.9 us (89%)
  local copies, waits for them, and re-layouts  8.98 us (9%)
  between operations  1.3 us (1%)
    pallas_call x1, Pallas kernels, on_device(): pl.pallas_call(functools.partial(kernel, dims, scale), out_shape=[jax.Sha...  92.9 us
    unnamed x19, local copies, waits for them, and re-layouts  8.9 us

profile of v1, /device:TPU:1, one launch (start us, length us, event | category | flops | bytes accessed | tf_op | source)
XLA Modules:
  0.0 103.2 jit_solution(5006762213552260299)
XLA Ops:
  1.3 0.0 copy-start.6
  1.3 0.7 copy-done.6
  2.0 0.1 bitcast_dynamic-update-slice_fusion
  2.1 0.1 broadcast_in_dim.11.idx_ref
  2.1 0.0 copy-start
  2.1 0.9 copy-done
  3.1 0.0 copy-start.1
  3.1 0.9 copy-done.1
  4.0 0.0 copy-start.2
  4.0 0.8 copy-done.2
  4.8 0.0 copy-start.3
  4.8 0.8 copy-done.3
  5.7 0.0 copy-start.4
  5.7 0.8 copy-done.4
  6.4 0.0 copy-start.5
  6.4 0.8 copy-done.5
  7.2 92.9 %shard_map.119 = (bf16[128,256]{1,0:T(8,128)(2,1)S(1)}, bf16[128,256]{1,0:T(8,128)(2,1)S(1)}, f32[64,256]{1,0:T(8,128)S(1)}, f32[64,256]{1,0:T(8,128)S(1)}, f32[384,128]{1,0:T(8,128)S(1)}) custom-call(bf16[128,256]{1,0:T(8,128)(2,1)S(1)} %copy-done.2, bf16[256,512]{1,0:T(8,128)(2,1)S(1)} %copy-done, bf16[3,128,128]{2,1,0:T(8,128)(2,1)S(1)} %copy-done.1, ...), custom_call_target="tpu_custom_call" | custom-call | tf_op jit(solution)/shard_map/pallas_call | solution.py:326
  100.0 0.6 copy.20
  100.7 0.6 copy.21
  101.3 0.7 copy.22
  102.0 0.6 copy.23
  102.6 0.6 copy.24
  (2 shorter events, 0.0 us)
Async XLA Ops:
  1.3 0.7 copy-start.6
  2.1 0.9 copy-start
  3.1 0.9 copy-start.1
  4.0 0.8 copy-start.2
  4.8 0.8 copy-start.3
  5.7 0.8 copy-start.4
  6.4 0.8 copy-start.5

commit v2 on v1

v2 whole, which is shorter than its diff:
```python
import functools

import jax
import jax.numpy as jnp
from jax import lax
from jax.experimental import pallas as pl
from jax.experimental.pallas import tpu as pltpu
from jax.sharding import PartitionSpec as P

MESH = pl.DeviceIdType.MESH
F32 = jnp.float32
BF16 = jnp.bfloat16
BLK = 128
NC = 2


def dot(a, b, ca, cb):
    return lax.dot_general(a, b, (((ca,), (cb,)), ((), ())), preferred_element_type=F32)


def kernel(
    dims, scale,
    x_in, w_in, blk_in, index_in, count_in, at_in, b_in, g_in,
    proj_ref, gradx_ref, grada_ref, gradb_ref, gradblk_ref,
    x_ref, w_ref, blk_ref, index_ref, count_ref, at_ref, b_ref, g_ref,
    wl, wq, xg, gz, orx, os_, gxr, gxs, gxacc, gss, gsr, up, ux, uz, ut, ug, idxg, bs, bx, br, tot, rss, rsr, agb, ab, gab,
    load_s, ring_s, ring_r, fwd_s, fwd_r, x_s, x_r, y_s, y_r, g_s, g_r, o_s, o_r, q_s, q_r, gs_s, gs_r,
    ux_s, ux_r, uz_s, uz_r, ug_s, ug_r, id_s, id_r, b_s, b_r, rs_s, rs_r, ag_s, ag_r,
):
    nx, ny, nz = dims
    nq = ny // nx
    nt = ny * NC
    half = ny // 2
    feat, tok = lax.axis_index("feat"), lax.axis_index("tok")
    x, z = feat // nz, feat % nz
    y, c = tok // NC, tok % NC
    zc = (z // 2) % 2
    zq, zh = z // (2 * NC), z % 2
    sib = 1 - c
    hb = x_ref.shape[0]
    pending = []

    def dev(xx, yy, zz, cc):
        return (xx * nz + zz, yy * NC + cc)

    def remote(src, dst, s_sem, r_sem, target):
        return pltpu.make_async_remote_copy(
            src_ref=src, dst_ref=dst, send_sem=s_sem, recv_sem=r_sem, device_id=target, device_id_type=MESH
        )

    def send(src, dst, s_sem, r_sem, target):
        copy = remote(src, dst, s_sem, r_sem, target)
        copy.start()
        pending.append((None, copy))

    def send_if(cond, src, dst, s_sem, r_sem, target):
        copy = remote(src, dst, s_sem, r_sem, target)
        pl.when(cond)(copy.start)
        pending.append((cond, copy))

    def send_or_keep(mine, src, dst, s_sem, r_sem, target):
        pl.when(mine)(pltpu.make_async_copy(src, dst, r_sem).start)
        send_if(jnp.logical_not(mine), src, dst, s_sem, r_sem, target)

    def arrived(dst, sem):
        pltpu.make_async_copy(dst, dst, sem).wait()

    barrier = pltpu.get_barrier_semaphore()
    greeted = 0
    for dz in range(1, nz):
        for cc in range(NC):
            pl.semaphore_signal(barrier, inc=1, device_id=dev(x, y, (z + dz) % nz, cc), device_id_type=MESH)
            greeted += 1
    for dt in range(1, nt):
        pl.semaphore_signal(barrier, inc=1, device_id=(feat, (tok + dt) % nt), device_id_type=MESH)
        greeted += 1
    for dx in range(1, nx):
        pl.semaphore_signal(barrier, inc=1, device_id=dev((x + dx) % nx, y, z, c), device_id_type=MESH)
        greeted += 1

    loads = []
    pairs = [
        (w_in, w_ref), (blk_in, blk_ref), (index_in, index_ref), (count_in, count_ref),
        (x_in, x_ref), (at_in, at_ref), (g_in, g_ref), (b_in, b_ref),
    ]
    for i, (src, dst) in enumerate(pairs):
        copy = pltpu.make_async_copy(src, dst, load_s.at[i])
        copy.start()
        loads.append(copy)
    for copy in loads[:4]:
        copy.wait()

    nsl = blk_ref.shape[0]
    for j in range(nsl):
        col = jnp.where(count_ref[...] > j, index_ref[1:2, j:j + 1], -1).astype(F32)
        idxg[x, j:j + 1, :] = jnp.broadcast_to(col, (1, BLK))
        idxg[x, 4 + j:5 + j, :] = jnp.broadcast_to(index_ref[0:1, j:j + 1].astype(F32), (1, BLK))
    for h in range(2):
        for rr in range(2):
            for hh in range(2):
                r0, c0 = rr * BLK, h * 2 * BLK + hh * BLK
                piece = w_ref[r0:r0 + BLK, c0:c0 + BLK].astype(F32)
                column = (tok * 4 + h * 2 + hh).astype(F32)
                for j in range(nsl):
                    hit = jnp.where(idxg[x, j:j + 1, :] == column, 1.0, 0.0) * jnp.where(
                        idxg[x, 4 + j:5 + j, :] == float(rr), 1.0, 0.0
                    )
                    piece = piece + hit * blk_ref[j].astype(F32)
                wl[0, h, r0:r0 + BLK, hh * BLK:(hh + 1) * BLK] = piece.astype(BF16)

    for copy in loads[4:]:
        copy.wait()
    rank = at_ref.shape[0]
    ab[...] = jnp.zeros_like(ab)
    ab[0, 0:rank, :] = at_ref[...]
    ab[1, rank:2 * rank, :] = b_ref[...]
    ab[2, 0:rank, :] = b_ref[...]
    ab[3, rank:2 * rank, :] = at_ref[...]
    part = (dot(x_ref[...], ab[0], 1, 1) + dot(g_ref[...], ab[1], 1, 1)).astype(BF16)
    ur = hb // nx
    for xx in range(nx):
        up[xx] = part[xx * ur:(xx + 1) * ur]

    pl.semaphore_wait(barrier, greeted)

    last = ny - 2

    def ring_slot(direction, k):
        d, sub = k // 2 + 1, (k + direction) % 2
        return (d if direction == 0 else half + d), d, sub

    def ring_send(direction, k):
        if k > last:
            return
        if k < 2:
            src = wl.at[0, (k + direction) % 2]
        else:
            slot, _, sub = ring_slot(direction, k - 2)
            src = wl.at[slot, sub]
        slot, _, sub = ring_slot(direction, k)
        to = (y + 1) % ny if direction == 0 else (y + ny - 1) % ny
        send(src, wl.at[slot, sub], ring_s.at[direction, k], ring_r.at[direction, k], dev(x, to, z, c))

    def hand_on(slot, sub, yy):
        xx, qq = yy // nq, yy % nq
        send_or_keep(
            x == xx, wl.at[slot, sub], wq.at[x, qq, sub], fwd_s.at[slot, sub], fwd_r.at[x, qq, sub], dev(xx, y, z, c)
        )

    def row_of(direction, d):
        return (y + ny - d) % ny if direction == 0 else (y + d) % ny

    def ring_step(k):
        for direction in range(2):
            slot, d, sub = ring_slot(direction, k)
            arrived(wl.at[slot, sub], ring_r.at[direction, k])
            ring_send(direction, k + 2)
            hand_on(slot, sub, row_of(direction, d))

    mine_rows = pl.ds(pl.multiple_of(c * hb, hb), hb)
    for k in range(2):
        for direction in range(2):
            ring_send(direction, k)
    for dx in range(1, nx):
        xx = (x + dx) % nx
        send(up.at[xx], ux.at[x], ux_s.at[dx], ux_r.at[x], dev(xx, y, z, c))
        send(idxg.at[x], idxg.at[x], id_s.at[dx], id_r.at[x], dev(xx, y, z, c))
    for dx in range(1, nx):
        send(x_ref, xg.at[x, mine_rows], x_s.at[dx], x_r.at[x], dev((x + dx) % nx, y, z, c))
    pltpu.make_async_copy(x_ref, xg.at[x, mine_rows], x_r.at[x]).start()
    for h in range(2):
        hand_on(0, h, y)

    def low_rank_over_z():
        total = up[x].astype(F32)
        for dx in range(1, nx):
            xx = (x + dx) % nx
            arrived(ux.at[xx], ux_r.at[xx])
            total = total + ux[xx].astype(F32)
        uz[z] = total.astype(BF16)
        for dz in range(1, nz):
            send(uz.at[z], uz.at[z], uz_s.at[dz], uz_r.at[z], dev(x, y, (z + dz) % nz, c))

    def cotangent_over_z():
        for dz in range(nz):
            args = (g_ref, gz.at[zq, zh, mine_rows], g_s.at[dz], g_r.at[zq, zh, c], dev(x, y, (z + dz) % nz, zc))
            if dz:
                send(*args)
            else:
                send_or_keep(c == zc, *args)

    def activations_on_chip():
        for dx in range(nx):
            xx = (x + dx) % nx
            arrived(xg.at[xx, mine_rows], x_r.at[xx])
            send(xg.at[xx, mine_rows], xg.at[xx, mine_rows], y_s.at[xx], y_r.at[xx], dev(x, y, z, sib))

    def low_rank_over_x():
        total = uz[z].astype(F32)
        for dz in range(1, nz):
            zz = (z + dz) % nz
            arrived(uz.at[zz], uz_r.at[zz])
            total = total + uz[zz].astype(F32)
        ut[x] = total.astype(BF16)
        for dx in range(1, nx):
            send(ut.at[x], ut.at[x], ug_s.at[dx], ug_r.at[x], dev((x + dx) % nx, y, z, c))

    def low_rank_done():
        for dx in range(1, nx):
            xx = (x + dx) % nx
            arrived(ut.at[xx], ug_r.at[xx])
        for xx in range(nx):
            ug[xx * ur:(xx + 1) * ur, :] = ut[xx]
        uv = ug[...]
        gab[0:rank] = dot(uv, g_ref[...], 0, 0)[0:rank]
        gab[rank:2 * rank] = dot(uv, x_ref[...], 0, 0)[rank:2 * rank]

    def blocks_over_x():
        other_rows = pl.ds(pl.multiple_of(sib * hb, hb), hb)
        for dx in range(nx):
            xx = (x + dx) % nx
            if dx:
                arrived(idxg.at[xx], id_r.at[xx])
            arrived(xg.at[xx, other_rows], y_r.at[xx])
        for qq in range(nq):
            for h in range(2):
                for cc in range(NC):
                    arrived(gz.at[qq, h, cc * hb:(cc + 1) * hb], g_r.at[qq, h, cc])
        for dx in range(nx):
            xx = (x + dx) % nx
            for j in range(nsl):
                col, row = idxg[xx, j:j + 1, :], idxg[xx, 4 + j:5 + j, :]
                picked = jnp.zeros((NC * hb, BLK), BF16)
                for qq in range(nq):
                    for h in range(2):
                        base = (2 * (x * nz + 4 * qq + 2 * c + h)).astype(F32)
                        for hh in range(2):
                            hit = jnp.where(col == base + float(hh), 1.0, 0.0).astype(BF16)
                            picked = picked + gz[qq, h, :, hh * BLK:(hh + 1) * BLK] * hit
                top = jnp.where(row == 0.0, 1.0, 0.0).astype(BF16)
                low = jnp.where(row == 1.0, 1.0, 0.0).astype(BF16)
                xs = xg[xx, :, 0:BLK] * top + xg[xx, :, BLK:2 * BLK] * low
                bs[dx, j * BLK:(j + 1) * BLK, :] = dot(xs, picked, 0, 0)

    ra, rb = 2 * rank // nt, nsl * BLK // nt

    def grads_over_tok():
        for tt in range(nt):
            rows = gab[tt * ra:(tt + 1) * ra]
            rss[tt, 0:2 * ra, :] = jnp.concatenate([rows[:, 0:BLK], rows[:, BLK:2 * BLK]], axis=0).astype(BF16)
            for dx in range(nx):
                r0 = 2 * ra + dx * rb
                rss[tt, r0:r0 + rb, :] = bs[dx, tt * rb:(tt + 1) * rb, :].astype(BF16)
        rsr[tok] = rss[tok]
        for dt in range(1, nt):
            tt = (tok + dt) % nt
            send(rss.at[tt], rsr.at[tok], rs_s.at[dt], rs_r.at[tok], (feat, tt))

    def blocks_home():
        total = rsr[tok].astype(F32)
        for dt in range(1, nt):
            tt = (tok + dt) % nt
            arrived(rsr.at[tt], rs_r.at[tt])
            total = total + rsr[tt].astype(F32)
        part = total[0:2 * ra]
        tot[0:2 * ra, :] = part
        for dx in range(nx):
            r0 = 2 * ra + dx * rb
            bx[dx] = total[r0:r0 + rb].astype(BF16)
            if dx:
                send(bx.at[dx], br.at[x], b_s.at[dx], b_r.at[x], dev((x + dx) % nx, y, z, c))
        tot[2 * ra:2 * ra + rb, :] = total[2 * ra:2 * ra + rb]

    def grads_back():
        total = tot[2 * ra:2 * ra + rb, :]
        for dx in range(1, nx):
            xx = (x + dx) % nx
            arrived(br.at[xx], b_r.at[xx])
            total = total + br[xx].astype(F32)
        tot[2 * ra:2 * ra + rb, :] = total
        agb[tok] = (tot[...] * scale).astype(BF16)
        for dt in range(1, nt):
            send(agb.at[tok], agb.at[tok], ag_s.at[dt], ag_r.at[tok], (feat, (tok + dt) % nt))

    def chunk(step):
        h = (step + z) % 2
        near = (y // nq - x) % nx < nx // 2
        qq = jnp.where(near, nq - 1 - step // 2, step // 2)
        for dx in range(nx):
            xx = (x + dx) % nx
            arrived(wq.at[xx, qq, h], fwd_r.at[xx, qq, h])
        out = dot(xg[0], wq[0, qq, h], 1, 0)
        for xx in range(1, nx):
            out = out + dot(xg[xx], wq[xx, qq, h], 1, 0)
        os_[step] = out.astype(BF16)
        zz = 4 * qq + 2 * c + h
        for cc in range(NC):
            send_or_keep(
                jnp.logical_and(z == zz, c == cc),
                os_.at[step, cc * hb:(cc + 1) * hb], orx.at[z], o_s.at[step, cc], o_r.at[z], dev(x, y, zz, cc),
            )
        for xx in range(nx):
            term = dot(gz[qq, h], wq[xx, qq, h], 1, 1)
            gxacc[xx] = term if step == 0 else gxacc[xx] + term

    def inputs_on_chip():
        other_rows = pl.ds(pl.multiple_of(sib * hb, hb), hb)
        gss[...] = gxacc[:, other_rows, :].astype(BF16)
        send(gss, gsr, gs_s.at[0], gs_r.at[0], dev(x, y, z, sib))

    def inputs_over_x():
        arrived(gsr, gs_r.at[0])
        for dx in range(nx):
            xx = (x + dx) % nx
            gxs[dx] = (gxacc[xx, mine_rows, :] + gsr[xx].astype(F32)).astype(BF16)
            if dx:
                send(gxs.at[dx], gxr.at[x], q_s.at[dx], q_r.at[x], dev(xx, y, z, c))

    low_rank_over_z()
    cotangent_over_z()
    after = {1: [activations_on_chip], 2: [low_rank_over_x]}
    for k in range(ny - 1):
        ring_step(k)
        for side in after.pop(k, []):
            side()
    for k in sorted(after):
        for side in after[k]:
            side()
    blocks_over_x()
    low_rank_done()
    grads_over_tok()
    for step in range(2 * nq):
        chunk(step)
        if step == nq - 1:
            blocks_home()
    inputs_on_chip()
    grads_back()
    inputs_over_x()

    uv = ug[...]
    out = dot(uv, ab[2], 1, 0)
    for zz in range(nz):
        arrived(orx.at[zz], o_r.at[zz])
        out = out + orx[zz].astype(F32)
    proj_ref[...] = out.astype(BF16)

    out = dot(uv, ab[3], 1, 0) + gxs[0].astype(F32)
    for dx in range(1, nx):
        xx = (x + dx) % nx
        arrived(gxr.at[xx], q_r.at[xx])
        out = out + gxr[xx].astype(F32)
    gradx_ref[...] = out.astype(BF16)

    for dt in range(1, nt):
        tt = (tok + dt) % nt
        arrived(agb.at[tt], ag_r.at[tt])
    for tt in range(nt):
        r0 = tt * ra
        ref, r0 = (gradb_ref, r0) if r0 < rank else (grada_ref, r0 - rank)
        back = agb[tt].astype(F32)
        ref[r0:r0 + ra, 0:BLK] = back[0:ra]
        ref[r0:r0 + ra, BLK:2 * BLK] = back[ra:2 * ra]
        gradblk_ref[tt * rb:(tt + 1) * rb, :] = back[2 * ra:2 * ra + rb]

    for cond, copy in pending:
        if cond is None:
            copy.wait_send()
        else:
            pl.when(cond)(copy.wait_send)


def write_out(*refs):
    n = 5
    load, store = refs[3 * n], refs[3 * n + 1]
    ins = [pltpu.make_async_copy(refs[i], refs[2 * n + i], load.at[i]) for i in range(n)]
    outs = [pltpu.make_async_copy(refs[2 * n + i], refs[n + i], store.at[i]) for i in range(n)]
    for copy in ins:
        copy.start()
    for i in range(n):
        ins[i].wait()
        outs[i].start()
    for copy in outs:
        copy.wait()


def make(dims):
    nx, ny, nz = dims
    nq, nt = ny // nx, ny * NC

    def on_device(activations, w_base, blk_vals, blk_index, blk_count, a_down, b_up, grad_out):
        hb, fb = activations.shape
        nsl, rank = blk_vals.shape[0], a_down.shape[1]
        scale = float(hb * nt) ** (-0.5)
        ra, rb = 2 * rank // nt, nsl * BLK // nt
        dma = pltpu.SemaphoreType.DMA
        vmem = pltpu.VMEM
        shapes = [
            jax.ShapeDtypeStruct((hb, fb), BF16),
            jax.ShapeDtypeStruct((hb, fb), BF16),
            jax.ShapeDtypeStruct((rank, fb), F32),
            jax.ShapeDtypeStruct((rank, fb), F32),
            jax.ShapeDtypeStruct((nsl * BLK, BLK), F32),
        ]
        results = pl.pallas_call(
            functools.partial(kernel, dims, scale),
            out_shape=shapes,
            in_specs=[pl.BlockSpec(memory_space=pltpu.HBM)] * 8,
            out_specs=[pl.BlockSpec(memory_space=vmem)] * 5,
            scratch_shapes=[
                vmem((hb, fb), BF16), vmem((fb, 2 * fb), BF16), vmem((nsl, BLK, BLK), BF16), vmem((2, nsl), jnp.int32),
                vmem((1, 1), jnp.int32), vmem((rank, fb), BF16), vmem((rank, fb), BF16), vmem((hb, fb), BF16),
                vmem((ny + 1, 2, fb, fb), BF16),
                vmem((nx, nq, 2, fb, fb), BF16),
                vmem((nx, NC * hb, fb), BF16),
                vmem((nq, 2, NC * hb, fb), BF16),
                vmem((nz, hb, fb), BF16),
                vmem((2 * nq, NC * hb, fb), BF16),
                vmem((nx, hb, fb), BF16),
                vmem((nx, hb, fb), BF16),
                vmem((nx, NC * hb, fb), F32),
                vmem((nx, hb, fb), BF16),
                vmem((nx, hb, fb), BF16),
                vmem((nx, hb // nx, 2 * rank), BF16),
                vmem((nx, hb // nx, 2 * rank), BF16),
                vmem((nz, hb // nx, 2 * rank), BF16),
                vmem((nx, hb // nx, 2 * rank), BF16),
                vmem((hb, 2 * rank), BF16),
                vmem((nx, 8, BLK), F32),
                vmem((nx, nsl * BLK, BLK), F32),
                vmem((nx, rb, BLK), BF16),
                vmem((nx, rb, BLK), BF16),
                vmem((2 * ra + rb, BLK), F32),
                vmem((nt, 2 * ra + nx * rb, BLK), BF16),
                vmem((nt, 2 * ra + nx * rb, BLK), BF16),
                vmem((nt, 2 * ra + rb, BLK), BF16),
                vmem((4, 2 * rank, fb), BF16),
                vmem((2 * rank, fb), F32),
                dma((8,)),
                dma((2, ny)), dma((2, ny)),
                dma((ny + 1, 2)), dma((nx, nq, 2)),
                dma((nx,)), dma((nx,)),
                dma((nx,)), dma((nx,)),
                dma((nz,)), dma((nq, 2, NC)),
                dma((2 * nq, NC)), dma((nz,)),
                dma((nx,)), dma((nx,)),
                dma((1,)), dma((1,)),
                dma((nx,)), dma((nx,)),
                dma((nz,)), dma((nz,)),
                dma((nx,)), dma((nx,)),
                dma((nx,)), dma((nx,)),
                dma((nx,)), dma((nx,)),
                dma((nt,)), dma((nt,)),
                dma((nt,)), dma((nt,)),
            ],
            compiler_params=pltpu.CompilerParams(
                collective_id=0, has_side_effects=True, vmem_limit_bytes=63 * 1024 * 1024
            ),
        )(activations, w_base, blk_vals, blk_index.T, blk_count.reshape(1, 1), a_down.T, b_up, grad_out)
        proj, gradx, grad_at, grad_b, blk = pl.pallas_call(
            write_out,
            out_shape=shapes,
            in_specs=[pl.BlockSpec(memory_space=pltpu.HBM)] * 5,
            out_specs=[pl.BlockSpec(memory_space=pltpu.HBM)] * 5,
            scratch_shapes=[vmem(s.shape, s.dtype) for s in shapes] + [dma((5,)), dma((5,))],
            compiler_params=pltpu.CompilerParams(vmem_limit_bytes=63 * 1024 * 1024),
        )(*results)
        return proj, gradx, blk.reshape(nsl, BLK, BLK), grad_at.T, grad_b

    return on_device


def solution(mesh, dims=(4, 8, 8)):
    in_specs = (
        P("tok", "feat"),
        P("feat", "tok"),
        P("feat", None, None),
        P("feat", None),
        P("feat"),
        P("feat", None),
        P(None, "feat"),
        P("tok", "feat"),
    )
    out_specs = (
        P("tok", "feat"),
        P("tok", "feat"),
        P("feat", None, None),
        P("feat", None),
        P(None, "feat"),
    )
    return jax.shard_map(make(dims), mesh=mesh, in_specs=in_specs, out_specs=out_specs, check_vma=False)
```

time: 104 us -> 75.5 us (0.73)
  Pallas kernels: 92.9 us -> 74 us
  local copies, waits for them, and re-layouts: 8.98 us -> 0 us
    pallas_call x1 -> x2, Pallas kernels: 92.9 us -> 74 us  [the longest x1 72.2 us: on_device(): pl.pallas_call(functools.partial(kernel, dims, scale), out_shape=shapes,...]
    unnamed x19 -> x0, local copies, waits for them, and re-layouts: 8.9 us -> none
where the time goes in v2:
time: 75.5 us; the launch traced here: 75.3 us
  Pallas kernels  74 us (98%)
  between operations  1.29 us (2%)
    pallas_call x1, Pallas kernels, on_device(): pl.pallas_call(functools.partial(kernel, dims, scale), out_shape=shapes,...  72.2 us
    pallas_call x1, Pallas kernels, on_device(): pl.pallas_call(write_out, out_shape=shapes, in_specs=[pl.BlockSpec(memory...  1.82 us

profile of v2, /device:TPU:1, one launch (start us, length us, event | category | flops | bytes accessed | tf_op | source)
XLA Modules:
  0.0 75.3 jit_solution(3842321874903662812)
XLA Ops:
  1.3 72.2 %shard_map.119 = (bf16[128,256]{1,0:T(8,128)(2,1)}, bf16[128,256]{1,0:T(8,128)(2,1)}, f32[64,256]{1,0:T(8,128)}, f32[64,256]{1,0:T(8,128)}, f32[384,128]{1,0:T(8,128)}) custom-call(bf16[128,256]{1,0:T(8,128)(2,1)} %x_in.1, bf16[256,512]{1,0:T(8,128)(2,1)} %w_in.1, bf16[3,128,128]{2,1,0:T(8,128)(2,1)} %blk_in.1, s32[2,3]{1,0:T(2,128)} %bitcast.7, ...), custom_call_target="tpu_custom_call" | custom-call | tf_op jit(solution)/shard_map/pallas_call | solution.py:404
  73.5 1.8 %shard_map.120 = (bf16[128,256]{1,0:T(8,128)(2,1)}, bf16[128,256]{1,0:T(8,128)(2,1)}, f32[64,256]{1,0:T(8,128)}, f32[64,256]{1,0:T(8,128)}, f32[384,128]{1,0:T(8,128)}) custom-call(bf16[128,256]{1,0:T(8,128)(2,1)} %get-tuple-element.15.refs_0_, bf16[128,256]{1,0:T(8,128)(2,1)} %get-tuple-element.16.refs_1_, f32[64,256]{1,0:T(8,128)} %get-tuple-element.17.refs_2_, ...), custom_call_target="tpu_custom_call" | custom-call | tf_op jit(solution)/shard_map/pallas_call | solution.py:459

commit v3 on v2

--- a/solution.py
+++ b/solution.py
@@ -23,9 +23,9 @@
     x_in, w_in, blk_in, index_in, count_in, at_in, b_in, g_in,
     proj_ref, gradx_ref, grada_ref, gradb_ref, gradblk_ref,
     x_ref, w_ref, blk_ref, index_ref, count_ref, at_ref, b_ref, g_ref,
-    wl, wq, xg, gz, orx, os_, gxr, gxs, gxacc, gss, gsr, up, ux, uz, ut, ug, idxg, bs, bx, br, tot, rss, rsr, agb, ab, gab,
-    load_s, ring_s, ring_r, fwd_s, fwd_r, x_s, x_r, y_s, y_r, g_s, g_r, o_s, o_r, q_s, q_r, gs_s, gs_r,
-    ux_s, ux_r, uz_s, uz_r, ug_s, ug_r, id_s, id_r, b_s, b_r, rs_s, rs_r, ag_s, ag_r,
+    wl, wq, xg, gz, orx, os_, gxr, gxs, gxacc, gss, gsr, up, ux, uz, ut, ug, idxg, bs, bss, bsr, gas, gar, bx, br, tot, rss, rsr, agb, ab, gab,
+    load_s, ring_s, ring_r, fwd_s, fwd_r, far_s, x_s, x_r, y_s, y_r, g_s, g_r, o_s, o_r, q_s, q_r, gs_s, gs_r,
+    ux_s, ux_r, uz_s, uz_r, ug_s, ug_r, id_s, id_r, bc_s, bc_r, b_s, b_r, rs_s, rs_r, ag_s, ag_r,
 ):
     nx, ny, nz = dims
     nq = ny // nx
@@ -75,8 +75,9 @@
         pl.semaphore_signal(barrier, inc=1, device_id=(feat, (tok + dt) % nt), device_id_type=MESH)
         greeted += 1
     for dx in range(1, nx):
-        pl.semaphore_signal(barrier, inc=1, device_id=dev((x + dx) % nx, y, z, c), device_id_type=MESH)
-        greeted += 1
+        for cc in range(NC):
+            pl.semaphore_signal(barrier, inc=1, device_id=dev((x + dx) % nx, y, z, cc), device_id_type=MESH)
+            greeted += 1
 
     loads = []
     pairs = [
@@ -141,11 +142,27 @@
         to = (y + 1) % ny if direction == 0 else (y + ny - 1) % ny
         send(src, wl.at[slot, sub], ring_s.at[direction, k], ring_r.at[direction, k], dev(x, to, z, c))
 
+    home = x == y // nq
+
     def hand_on(slot, sub, yy):
         xx, qq = yy // nq, yy % nq
+        if far(slot, sub):
+            pl.when(x == xx)(pltpu.make_async_copy(wl.at[slot, sub], wq.at[x, qq, sub], fwd_r.at[x, qq, sub]).start)
+            return
         send_or_keep(
             x == xx, wl.at[slot, sub], wq.at[x, qq, sub], fwd_s.at[slot, sub], fwd_r.at[x, qq, sub], dev(xx, y, z, c)
         )
+
+    def far(slot, sub):
+        return nx == 4 and slot == 2 * half and sub == 1
+
+    def to_far_row():
+        qq = y % nq
+        for dx in range(1, nx):
+            xx = (x + dx) % nx
+            piece = wq.at[xx, qq, 1]
+            pl.when(home)(pltpu.make_async_copy(piece, piece, fwd_r.at[xx, qq, 1]).wait)
+            send_if(home, piece, piece, far_s.at[dx], fwd_r.at[xx, qq, 1], dev(x, (y + half) % ny, z, c))
 
     def row_of(direction, d):
         return (y + ny - d) % ny if direction == 0 else (y + d) % ny
@@ -155,7 +172,12 @@
             slot, d, sub = ring_slot(direction, k)
             arrived(wl.at[slot, sub], ring_r.at[direction, k])
             ring_send(direction, k + 2)
-            hand_on(slot, sub, row_of(direction, d))
+            if k != ny - 3:
+                hand_on(slot, sub, row_of(direction, d))
+        if k == ny - 2 and k:
+            for direction in range(2):
+                slot, d, sub = ring_slot(direction, k - 1)
+                hand_on(slot, sub, row_of(direction, d))
 
     mine_rows = pl.ds(pl.multiple_of(c * hb, hb), hb)
     for k in range(2):
@@ -181,8 +203,8 @@
         for dz in range(1, nz):
             send(uz.at[z], uz.at[z], uz_s.at[dz], uz_r.at[z], dev(x, y, (z + dz) % nz, c))
 
-    def cotangent_over_z():
-        for dz in range(nz):
+    def cotangent_over_z(distances):
+        for dz in distances:
             args = (g_ref, gz.at[zq, zh, mine_rows], g_s.at[dz], g_r.at[zq, zh, c], dev(x, y, (z + dz) % nz, zc))
             if dz:
                 send(*args)
@@ -242,39 +264,56 @@
                 xs = xg[xx, :, 0:BLK] * top + xg[xx, :, BLK:2 * BLK] * low
                 bs[dx, j * BLK:(j + 1) * BLK, :] = dot(xs, picked, 0, 0)
 
-    ra, rb = 2 * rank // nt, nsl * BLK // nt
+    ra, rb = rank // ny, nsl * BLK // nt
+    hx = nx // NC
+
+    def blocks_on_chip():
+        for i in range(hx):
+            bss[i] = bs[sib * hx + i].astype(BF16)
+        send(bss, bsr, bc_s.at[0], bc_r.at[0], dev(x, y, z, sib))
+
+    def low_rank_on_chip():
+        gas[...] = gab[pl.ds(pl.multiple_of(sib * rank, rank), rank)].astype(BF16)
+        send(gas, gar, bc_s.at[1], bc_r.at[1], dev(x, y, z, sib))
 
     def grads_over_tok():
-        for tt in range(nt):
-            rows = gab[tt * ra:(tt + 1) * ra]
-            rss[tt, 0:2 * ra, :] = jnp.concatenate([rows[:, 0:BLK], rows[:, BLK:2 * BLK]], axis=0).astype(BF16)
-            for dx in range(nx):
-                r0 = 2 * ra + dx * rb
-                rss[tt, r0:r0 + rb, :] = bs[dx, tt * rb:(tt + 1) * rb, :].astype(BF16)
-        rsr[tok] = rss[tok]
-        for dt in range(1, nt):
-            tt = (tok + dt) % nt
-            send(rss.at[tt], rsr.at[tok], rs_s.at[dt], rs_r.at[tok], (feat, tt))
+        arrived(bsr, bc_r.at[0])
+        for i in range(hx):
+            rows = bs[c * hx + i] + bsr[i].astype(F32)
+            for yy in range(ny):
+                r0 = 2 * ra + i * NC * rb
+                rss[yy, r0:r0 + NC * rb, :] = rows[yy * NC * rb:(yy + 1) * NC * rb].astype(BF16)
+        arrived(gar, bc_r.at[1])
+        sums = gab[pl.ds(pl.multiple_of(c * rank, rank), rank)] + gar[...].astype(F32)
+        for yy in range(ny):
+            rows = sums[yy * ra:(yy + 1) * ra]
+            rss[yy, 0:2 * ra, :] = jnp.concatenate([rows[:, 0:BLK], rows[:, BLK:2 * BLK]], axis=0).astype(BF16)
+        rsr[y] = rss[y]
+        for dy in range(1, ny):
+            yy = (y + dy) % ny
+            send(rss.at[yy], rsr.at[y], rs_s.at[dy], rs_r.at[y], dev(x, yy, z, c))
 
     def blocks_home():
-        total = rsr[tok].astype(F32)
-        for dt in range(1, nt):
-            tt = (tok + dt) % nt
-            arrived(rsr.at[tt], rs_r.at[tt])
-            total = total + rsr[tt].astype(F32)
-        part = total[0:2 * ra]
-        tot[0:2 * ra, :] = part
-        for dx in range(nx):
-            r0 = 2 * ra + dx * rb
-            bx[dx] = total[r0:r0 + rb].astype(BF16)
-            if dx:
-                send(bx.at[dx], br.at[x], b_s.at[dx], b_r.at[x], dev((x + dx) % nx, y, z, c))
-        tot[2 * ra:2 * ra + rb, :] = total[2 * ra:2 * ra + rb]
+        total = rsr[y].astype(F32)
+        for dy in range(1, ny):
+            yy = (y + dy) % ny
+            arrived(rsr.at[yy], rs_r.at[yy])
+            total = total + rsr[yy].astype(F32)
+        tot[0:2 * ra, :] = total[0:2 * ra]
+        for i in range(hx):
+            xx = (x + c * hx + i) % nx
+            for cc in range(NC):
+                r0 = 2 * ra + (i * NC + cc) * rb
+                bx[i, cc] = total[r0:r0 + rb].astype(BF16)
+                args = (bx.at[i, cc], br.at[x], b_s.at[i, cc], b_r.at[x], dev(xx, y, z, cc))
+                if i == 0 and cc == 0:
+                    send_or_keep(c == 0, *args)
+                else:
+                    send(*args)
 
     def grads_back():
-        total = tot[2 * ra:2 * ra + rb, :]
-        for dx in range(1, nx):
-            xx = (x + dx) % nx
+        total = jnp.zeros((rb, BLK), F32)
+        for xx in range(nx):
             arrived(br.at[xx], b_r.at[xx])
             total = total + br[xx].astype(F32)
         tot[2 * ra:2 * ra + rb, :] = total
@@ -283,12 +322,20 @@
             send(agb.at[tok], agb.at[tok], ag_s.at[dt], ag_r.at[tok], (feat, (tok + dt) % nt))
 
     def chunk(step):
-        h = (step + z) % 2
-        near = (y // nq - x) % nx < nx // 2
-        qq = jnp.where(near, nq - 1 - step // 2, step // 2)
+        if nq == 1:
+            qq, h = 0, step
+        elif step % 2:
+            qq, h = y % 2, step // 2
+        else:
+            qq, h = 1 - y % 2, (y + step // 2) % 2
+        early = jnp.logical_and(home, jnp.logical_and(qq == y % nq, h == 1)) if nx == 4 else None
         for dx in range(nx):
             xx = (x + dx) % nx
-            arrived(wq.at[xx, qq, h], fwd_r.at[xx, qq, h])
+            piece = wq.at[xx, qq, h]
+            if dx and nx == 4:
+                pl.when(jnp.logical_not(early))(pltpu.make_async_copy(piece, piece, fwd_r.at[xx, qq, h]).wait)
+            else:
+                arrived(piece, fwd_r.at[xx, qq, h])
         out = dot(xg[0], wq[0, qq, h], 1, 0)
         for xx in range(1, nx):
             out = out + dot(xg[xx], wq[xx, qq, h], 1, 0)
@@ -316,9 +363,11 @@
             if dx:
                 send(gxs.at[dx], gxr.at[x], q_s.at[dx], q_r.at[x], dev(xx, y, z, c))
 
+    around = sorted(range(nz), key=lambda dz: -min(dz, nz - dz))
+    cotangent_over_z(around[:3])
     low_rank_over_z()
-    cotangent_over_z()
-    after = {1: [activations_on_chip], 2: [low_rank_over_x]}
+    cotangent_over_z(around[3:])
+    after = {1: [activations_on_chip], 2: [low_rank_over_x], ny - 4: [to_far_row] if nx == 4 else []}
     for k in range(ny - 1):
         ring_step(k)
         for side in after.pop(k, []):
@@ -327,7 +376,9 @@
         for side in after[k]:
             side()
     blocks_over_x()
+    blocks_on_chip()
     low_rank_done()
+    low_rank_on_chip()
     grads_over_tok()
     for step in range(2 * nq):
         chunk(step)
@@ -355,8 +406,7 @@
         tt = (tok + dt) % nt
         arrived(agb.at[tt], ag_r.at[tt])
     for tt in range(nt):
-        r0 = tt * ra
-        ref, r0 = (gradb_ref, r0) if r0 < rank else (grada_ref, r0 - rank)
+        ref, r0 = (grada_ref if tt % NC else gradb_ref), tt // NC * ra
         back = agb[tt].astype(F32)
         ref[r0:r0 + ra, 0:BLK] = back[0:ra]
         ref[r0:r0 + ra, BLK:2 * BLK] = back[ra:2 * ra]
@@ -391,7 +441,7 @@
         hb, fb = activations.shape
         nsl, rank = blk_vals.shape[0], a_down.shape[1]
         scale = float(hb * nt) ** (-0.5)
-        ra, rb = 2 * rank // nt, nsl * BLK // nt
+        ra, rb = rank // ny, nsl * BLK // nt
         dma = pltpu.SemaphoreType.DMA
         vmem = pltpu.VMEM
         shapes = [
@@ -427,17 +477,22 @@
                 vmem((hb, 2 * rank), BF16),
                 vmem((nx, 8, BLK), F32),
                 vmem((nx, nsl * BLK, BLK), F32),
-                vmem((nx, rb, BLK), BF16),
+                vmem((nx // NC, nsl * BLK, BLK), BF16),
+                vmem((nx // NC, nsl * BLK, BLK), BF16),
+                vmem((rank, fb), BF16),
+                vmem((rank, fb), BF16),
+                vmem((nx // NC, NC, rb, BLK), BF16),
                 vmem((nx, rb, BLK), BF16),
                 vmem((2 * ra + rb, BLK), F32),
-                vmem((nt, 2 * ra + nx * rb, BLK), BF16),
-                vmem((nt, 2 * ra + nx * rb, BLK), BF16),
+                vmem((ny, 2 * ra + nx * rb, BLK), BF16),
+                vmem((ny, 2 * ra + nx * rb, BLK), BF16),
                 vmem((nt, 2 * ra + rb, BLK), BF16),
                 vmem((4, 2 * rank, fb), BF16),
                 vmem((2 * rank, fb), F32),
                 dma((8,)),
                 dma((2, ny)), dma((2, ny)),
                 dma((ny + 1, 2)), dma((nx, nq, 2)),
+                dma((nx,)),
                 dma((nx,)), dma((nx,)),
                 dma((nx,)), dma((nx,)),
                 dma((nz,)), dma((nq, 2, NC)),
@@ -448,8 +503,9 @@
                 dma((nz,)), dma((nz,)),
                 dma((nx,)), dma((nx,)),
                 dma((nx,)), dma((nx,)),
-                dma((nx,)), dma((nx,)),
-                dma((nt,)), dma((nt,)),
+                dma((2,)), dma((2,)),
+                dma((nx // NC, NC)), dma((nx,)),
+                dma((ny,)), dma((ny,)),
                 dma((nt,)), dma((nt,)),
             ],
             compiler_params=pltpu.CompilerParams(

time: 75.5 us -> 73.3 us (0.971)
  the two profiles are of different devices: /device:TPU:1 before, /device:TPU:9 now
where the time goes in v3:
time: 73.3 us; the launch traced here: 73.1 us
  Pallas kernels  71.8 us (98%)
  between operations  1.29 us (2%)
    pallas_call x1, Pallas kernels, on_device(): pl.pallas_call(functools.partial(kernel, dims, scale), out_shape=shapes,...  70 us
    pallas_call x1, Pallas kernels, on_device(): pl.pallas_call(write_out, out_shape=shapes, in_specs=[pl.BlockSpec(memory...  1.82 us

profile of v3, /device:TPU:9, one launch (start us, length us, event | category | flops | bytes accessed | tf_op | source)
XLA Modules:
  0.0 73.1 jit_solution(6559124685913581453)
XLA Ops:
  1.3 70.0 %shard_map.119 = (bf16[128,256]{1,0:T(8,128)(2,1)}, bf16[128,256]{1,0:T(8,128)(2,1)}, f32[64,256]{1,0:T(8,128)}, f32[64,256]{1,0:T(8,128)}, f32[384,128]{1,0:T(8,128)}) custom-call(bf16[128,256]{1,0:T(8,128)(2,1)} %x_in.1, bf16[256,512]{1,0:T(8,128)(2,1)} %w_in.1, bf16[3,128,128]{2,1,0:T(8,128)(2,1)} %blk_in.1, s32[2,3]{1,0:T(2,128)} %bitcast.7, ...), custom_call_target="tpu_custom_call" | custom-call | tf_op jit(solution)/shard_map/pallas_call | solution.py:454
  71.3 1.8 %shard_map.120 = (bf16[128,256]{1,0:T(8,128)(2,1)}, bf16[128,256]{1,0:T(8,128)(2,1)}, f32[64,256]{1,0:T(8,128)}, f32[64,256]{1,0:T(8,128)}, f32[384,128]{1,0:T(8,128)}) custom-call(bf16[128,256]{1,0:T(8,128)(2,1)} %get-tuple-element.15.refs_0_, bf16[128,256]{1,0:T(8,128)(2,1)} %get-tuple-element.16.refs_1_, f32[64,256]{1,0:T(8,128)} %get-tuple-element.17.refs_2_, ...), custom_call_target="tpu_custom_call" | custom-call | tf_op jit(solution)/shard_map/pallas_call | solution.py:515

commit v4 on v3

--- a/solution.py
+++ b/solution.py
@@ -324,10 +324,13 @@
     def chunk(step):
         if nq == 1:
             qq, h = 0, step
-        elif step % 2:
-            qq, h = y % 2, step // 2
         else:
-            qq, h = 1 - y % 2, (y + step // 2) % 2
+            away = (x + nx - y // nq) % nx
+            first = jnp.where(away == 2, 1 - y % 2, jnp.where(away == 3, 1, 0))
+            if step % 2:
+                qq, h = 1 - first, (jnp.where(away == 1, 1, 0) + step // 2) % 2
+            else:
+                qq, h = first, (jnp.where(away == 2, y % 2, 0) + step // 2) % 2
         early = jnp.logical_and(home, jnp.logical_and(qq == y % nq, h == 1)) if nx == 4 else None
         for dx in range(nx):
             xx = (x + dx) % nx
@@ -367,7 +370,7 @@
     cotangent_over_z(around[:3])
     low_rank_over_z()
     cotangent_over_z(around[3:])
-    after = {1: [activations_on_chip], 2: [low_rank_over_x], ny - 4: [to_far_row] if nx == 4 else []}
+    after = {1: [activations_on_chip], 2: [low_rank_over_x], ny - 4: [to_far_row] if nx == 4 else [], ny - 3: [blocks_over_x, blocks_on_chip]}
     for k in range(ny - 1):
         ring_step(k)
         for side in after.pop(k, []):
@@ -375,8 +378,6 @@
     for k in sorted(after):
         for side in after[k]:
             side()
-    blocks_over_x()
-    blocks_on_chip()
     low_rank_done()
     low_rank_on_chip()
     grads_over_tok()

time: 73.3 us -> 71.2 us (0.971)
  the two profiles are of different devices: /device:TPU:9 before, /device:TPU:1 now
where the time goes in v4:
time: 71.2 us; the launch traced here: 71 us
  Pallas kernels  69.7 us (98%)
  between operations  1.29 us (2%)
    pallas_call x1, Pallas kernels, on_device(): pl.pallas_call(functools.partial(kernel, dims, scale), out_shape=shapes,...  67.9 us
    pallas_call x1, Pallas kernels, on_device(): pl.pallas_call(write_out, out_shape=shapes, in_specs=[pl.BlockSpec(memory...  1.82 us

profile of v4, /device:TPU:1, one launch (start us, length us, event | category | flops | bytes accessed | tf_op | source)
XLA Modules:
  0.0 71.0 jit_solution(11032341243818355388)
XLA Ops:
  1.3 67.9 %shard_map.119 = (bf16[128,256]{1,0:T(8,128)(2,1)}, bf16[128,256]{1,0:T(8,128)(2,1)}, f32[64,256]{1,0:T(8,128)}, f32[64,256]{1,0:T(8,128)}, f32[384,128]{1,0:T(8,128)}) custom-call(bf16[128,256]{1,0:T(8,128)(2,1)} %x_in.1, bf16[256,512]{1,0:T(8,128)(2,1)} %w_in.1, bf16[3,128,128]{2,1,0:T(8,128)(2,1)} %blk_in.1, s32[2,3]{1,0:T(2,128)} %bitcast.7, ...), custom_call_target="tpu_custom_call" | custom-call | tf_op jit(solution)/shard_map/pallas_call | solution.py:455
  69.2 1.8 %shard_map.120 = (bf16[128,256]{1,0:T(8,128)(2,1)}, bf16[128,256]{1,0:T(8,128)(2,1)}, f32[64,256]{1,0:T(8,128)}, f32[64,256]{1,0:T(8,128)}, f32[384,128]{1,0:T(8,128)}) custom-call(bf16[128,256]{1,0:T(8,128)(2,1)} %get-tuple-element.15.refs_0_, bf16[128,256]{1,0:T(8,128)(2,1)} %get-tuple-element.16.refs_1_, f32[64,256]{1,0:T(8,128)} %get-tuple-element.17.refs_2_, ...), custom_call_target="tpu_custom_call" | custom-call | tf_op jit(solution)/shard_map/pallas_call | solution.py:516

commit v5 on v4

--- a/solution.py
+++ b/solution.py
@@ -385,8 +385,8 @@
         chunk(step)
         if step == nq - 1:
             blocks_home()
+    grads_back()
     inputs_on_chip()
-    grads_back()
     inputs_over_x()
 
     uv = ug[...]

time: 71.2 us -> 71.2 us (level)
  no operation moved by 1% of the time
where the time goes in v5:
time: 71.2 us; the launch traced here: 71 us
  Pallas kernels  69.7 us (98%)
  between operations  1.29 us (2%)
    pallas_call x1, Pallas kernels, on_device(): pl.pallas_call(functools.partial(kernel, dims, scale), out_shape=shapes,...  67.9 us
    pallas_call x1, Pallas kernels, on_device(): pl.pallas_call(write_out, out_shape=shapes, in_specs=[pl.BlockSpec(memory...  1.82 us

profile of v5, /device:TPU:1, one launch (start us, length us, event | category | flops | bytes accessed | tf_op | source)
XLA Modules:
  0.0 71.0 jit_solution(17527200788302530225)
XLA Ops:
  1.3 67.9 %shard_map.119 = (bf16[128,256]{1,0:T(8,128)(2,1)}, bf16[128,256]{1,0:T(8,128)(2,1)}, f32[64,256]{1,0:T(8,128)}, f32[64,256]{1,0:T(8,128)}, f32[384,128]{1,0:T(8,128)}) custom-call(bf16[128,256]{1,0:T(8,128)(2,1)} %x_in.1, bf16[256,512]{1,0:T(8,128)(2,1)} %w_in.1, bf16[3,128,128]{2,1,0:T(8,128)(2,1)} %blk_in.1, s32[2,3]{1,0:T(2,128)} %bitcast.7, ...), custom_call_target="tpu_custom_call" | custom-call | tf_op jit(solution)/shard_map/pallas_call | solution.py:455
  69.2 1.8 %shard_map.120 = (bf16[128,256]{1,0:T(8,128)(2,1)}, bf16[128,256]{1,0:T(8,128)(2,1)}, f32[64,256]{1,0:T(8,128)}, f32[64,256]{1,0:T(8,128)}, f32[384,128]{1,0:T(8,128)}) custom-call(bf16[128,256]{1,0:T(8,128)(2,1)} %get-tuple-element.15.refs_0_, bf16[128,256]{1,0:T(8,128)(2,1)} %get-tuple-element.16.refs_1_, f32[64,256]{1,0:T(8,128)} %get-tuple-element.17.refs_2_, ...), custom_call_target="tpu_custom_call" | custom-call | tf_op jit(solution)/shard_map/pallas_call | solution.py:516
